TPU v7x, 32 devices: a whole 2x2x4 slice. The times are simulated.
32 devices in a mesh: vol: 4 (over y, x), orient: 4 (over z), dp: 2 (over core).
Axes of the slice: x: 2, y: 2, z: 4, core: 2. Of those that a mesh axis runs over, the one named last changes fastest.
Arguments:
- volume: float32 [128, 65, 2, 8, 128], P('vol'), may hold values from -6 to 6
- weight_bank: float32 [64, 128, 128], replicated, may hold values from -3 to 3
- tile_slab: int32 [128, 65, 1], P(('vol', 'orient')), may hold values from 0 to 3; in each aligned block of 520 rows (0 to 519, 520 to 1039, ..., all dimensions but the last counted through in order) at most 260 rows name the same one
- tile_plane: int32 [128, 65], P(('vol', 'orient')), may hold values from 0 to 31
- tile_weight: int32 [128, 65], P(('vol', 'orient')), may hold values from 0 to 63
- particles: float32 [256, 65, 2, 128], P('dp'), may hold values from -6 to 6
- ctf: float32 [256, 65, 128], P('dp'), may hold values from -1 to 1
- noise_weight: float32 [65, 128], replicated, may hold values from 0.002 to 0.11
- offsets: int32 [256, 2], P('dp'), may hold values from -3 to 3
- earlier_class: int32 [256], P('dp'), may hold values from 0 to 7
- pose_free_term: float32 [256], P('dp'), may hold values from -160 to 160
Outputs:
- numerator: float32 [128, 65, 3, 8, 128], P(('vol', 'orient', 'dp'))
- posterior: float32 [256, 8], P('dp')
- log_evidence: float32 [256], P('dp')
Inputs may be any that keep to these rules, and one draw needn't show every extreme that they name: `tile_slab`: among the 65 tiles of the 8 poses of one device at most 260 name one slab, and in every draw some device's tiles name some slab exactly 260 times.
All inputs are finite; a program needn't handle non-finite values.
Results may differ from a plain program's by a relative error of at most 0.0003.
Values sent between devices are 32-bit elements; how exact they have to be, the bound alone decides.
No kernel may reach another device: no remote copies, remote signals or barrier semaphores. Data moves between devices by JAX's collectives and lax.ppermute only.
A program may use at most 192 MiB of HBM per device.

v0:
```python
import math
import jax
import jax.numpy as jnp
from jax import lax
from jax.sharding import PartitionSpec as P

SIDE = 128
NTRANS = 9
PREVIOUS_REWARD = 1.5
PRECISE = lax.Precision.HIGHEST


def pixel_frequencies(image_side, tile_count, tile_width):
    pixel = jnp.arange(tile_count * tile_width, dtype=jnp.int32).reshape(tile_count, tile_width)
    half_width = image_side // 2 + 1
    freq_x = pixel % half_width
    row_index = pixel // half_width
    freq_y = jnp.where(row_index < image_side // 2, row_index, row_index - image_side)
    return (freq_x, freq_y)


def moved_images(images, offsets, freq_x, freq_y, image_side, trans_step):
    shift_horizontal = offsets[:, 0] + (trans_step % 3 - 1)
    move_y = offsets[:, 1] + (trans_step // 3 - 1)
    turns = jnp.mod(
        freq_x[None] * shift_horizontal[:, None, None] + freq_y[None] * move_y[:, None, None],
        image_side,
    )
    phase_angle = turns.astype(jnp.float32) * (2.0 * math.pi / image_side)
    cosine = jnp.cos(phase_angle)
    sine_part = jnp.sin(phase_angle)
    real_part = images[:, :, 0, :]
    imag_part = images[:, :, 1, :]
    return jnp.stack(
        [real_part * cosine + imag_part * sine_part, imag_part * cosine - real_part * sine_part],
        axis=2,
    )


def project_tiles(blocks, weight_bank, chosen):
    matrices = weight_bank[chosen]
    return jnp.einsum("nckr,nrq->nckq", blocks, matrices, precision=PRECISE)


def back_project(tile_rows, weight_bank, chosen):
    matrices = weight_bank[chosen]
    return jnp.einsum("nmkq,nrq->nmkr", tile_rows, matrices, precision=PRECISE)


def shards(
    volume,
    weight_bank,
    tile_slab,
    tile_plane,
    tile_weight,
    particles,
    ctf,
    noise_weight,
    offsets,
    earlier_class,
    pose_free_term,
):
    slab_count = lax.axis_size("vol")
    pose_local = tile_plane.shape[0]
    tile_count = tile_plane.shape[1]
    tile_width = particles.shape[3]
    class_labels = volume.shape[3]
    planes = volume.shape[0]
    capacity = max(2, 2 * pose_local * tile_count // slab_count)
    row_total = pose_local * tile_count
    slab_of = tile_slab[:, :, 0].reshape(row_total)
    plane_of = tile_plane.reshape(row_total)
    chosen = tile_weight.reshape(row_total)
    target = (slab_of[:, None] == jnp.arange(slab_count, dtype=jnp.int32)[None]).astype(jnp.int32)
    slot_rank = jnp.sum((jnp.cumsum(target, axis=0) - 1) * target, axis=1)
    slot_index = slab_of * capacity + slot_rank
    local_cell = plane_of * tile_count + jnp.tile(
        jnp.arange(tile_count, dtype=jnp.int32), pose_local
    )
    request = jnp.full((slab_count * capacity,), -1, jnp.int32).at[slot_index].set(local_cell)
    request = request.reshape(slab_count, capacity)
    flat_volume = volume.reshape(planes * tile_count, 2, class_labels, tile_width)

    def project_group(item_pair):
        return project_tiles(item_pair[0], weight_bank, item_pair[1])

    def spread_group(item_pair):
        return back_project(item_pair[0], weight_bank, item_pair[1])

    weight_request = jnp.zeros((slab_count * capacity,), jnp.int32).at[slot_index].set(chosen)
    weight_request = weight_request.reshape(slab_count, capacity)
    incoming, incoming_weight = (
        lax.all_to_all(request, "vol", split_axis=0, concat_axis=0, tiled=True),
        lax.all_to_all(weight_request, "vol", split_axis=0, concat_axis=0, tiled=True),
    )
    is_valid = incoming >= 0
    picked = flat_volume[jnp.maximum(incoming, 0)]
    blocks = jnp.where(is_valid[..., None, None, None], picked, 0.0)
    pieces = lax.map(project_group, (blocks, incoming_weight))
    returned = lax.all_to_all(pieces, "vol", split_axis=0, concat_axis=0, tiled=True)
    slices = returned.reshape(slab_count * capacity, 2, class_labels, tile_width)[slot_index]
    slices = slices.reshape(pose_local, tile_count, 2, class_labels, tile_width)
    freq_x, freq_y = pixel_frequencies(SIDE, tile_count, tile_width)
    ctf_noise = noise_weight[None] * ctf
    power = jnp.sum(slices * slices, axis=2)
    norm_term = jnp.einsum("itq,ptkq->ikp", ctf_noise * ctf, power, precision=PRECISE)
    trans_steps = jnp.arange(NTRANS, dtype=jnp.int32)

    def score_step(trans_step):
        moved = moved_images(particles, offsets, freq_x, freq_y, SIDE, trans_step)
        return jnp.einsum(
            "itcq,ptckq->ikp", ctf_noise[:, :, None, :] * moved, slices, precision=PRECISE
        )

    cross_term = lax.map(score_step, trans_steps)
    earlier_class_term = jnp.where(
        earlier_class[:, None] == jnp.arange(class_labels, dtype=jnp.int32)[None],
        PREVIOUS_REWARD,
        0.0,
    )
    earlier_class_term = earlier_class_term + pose_free_term[:, None]
    scores = 2.0 * cross_term - norm_term[None] + earlier_class_term[None, :, :, None]
    peak_value = lax.pmax(jnp.max(scores, axis=(0, 2, 3)), ("vol", "orient"))
    exp_scores = jnp.exp(scores - peak_value[None, :, None, None])
    class_mass = lax.psum(jnp.sum(exp_scores, axis=(0, 3)), ("vol", "orient"))
    mass_total = jnp.sum(class_mass, axis=1)
    posterior = class_mass / mass_total[:, None]
    evidence = peak_value + jnp.log(mass_total)
    pose_count = pose_local * lax.axis_size("vol") * lax.axis_size("orient")
    post_share = exp_scores * (pose_count / mass_total)[None, :, None, None]

    def add_step(running, item_pair):
        trans_step, share_step = item_pair
        moved = moved_images(particles, offsets, freq_x, freq_y, SIDE, trans_step)
        term = jnp.einsum(
            "ikp,itcq->ptckq", share_step, ctf[:, :, None, :] * moved, precision=PRECISE
        )
        return (running + term, None)

    start = jnp.zeros((pose_local, tile_count, 2, class_labels, tile_width), jnp.float32)
    data_rows = lax.scan(add_step, start, (trans_steps, post_share))[0]
    weight_rows = jnp.einsum(
        "ikp,itq->ptkq", jnp.sum(post_share, axis=0), ctf * ctf, precision=PRECISE
    )
    slice_rows = jnp.concatenate([data_rows, weight_rows[:, :, None]], axis=2)
    outgoing = jnp.zeros((slab_count * capacity, 3, class_labels, tile_width), jnp.float32)
    outgoing = outgoing.at[slot_index].set(
        slice_rows.reshape(row_total, 3, class_labels, tile_width)
    )
    outgoing = outgoing.reshape(slab_count, capacity, 3, class_labels, tile_width)
    arrived_rows = lax.all_to_all(outgoing, "vol", split_axis=0, concat_axis=0, tiled=True)
    arrived = lax.map(spread_group, (arrived_rows, incoming_weight))
    cell_index = jnp.maximum(incoming, 0).reshape(-1)
    accumulated = jnp.zeros((planes * tile_count, 3, class_labels, tile_width), jnp.float32)
    accumulated = accumulated.at[cell_index].add(arrived.reshape(-1, 3, class_labels, tile_width))
    accumulated = accumulated.reshape(planes, tile_count, 3, class_labels, tile_width)
    numerator = lax.psum_scatter(accumulated, ("orient", "dp"), scatter_dimension=0, tiled=True)
    return (numerator, posterior, evidence)


def solution(mesh):
    in_specs = (
        P("vol", None, None, None, None),
        P(),
        P(("vol", "orient"), None, None),
        P(("vol", "orient"), None),
        P(("vol", "orient"), None),
        P("dp", None, None, None),
        P("dp", None, None),
        P(),
        P("dp", None),
        P("dp"),
        P("dp"),
    )
    out_specs = (P(("vol", "orient", "dp"), None, None, None, None), P("dp", None), P("dp"))
    return jax.shard_map(shards, mesh=mesh, in_specs=in_specs, out_specs=out_specs, check_vma=False)
```

profile of v0, /device:TPU:0, one launch (start us, length us, event | category | flops | bytes accessed | tf_op | source)
XLA Modules:
  0.0 1769.5 jit_solution(17040077565508846166)
XLA Ops:
  52.4 129.7 %while.52 = (s32[]{:T(128)}, f32[4,260,2,8,128]{4,3,2,1,0:T(8,128)}, f32[4,260,2,8,128]{4,3,2,1,0:T(8,128)}, s32[4,260]{1,0:T(4,128)S(1)}, f32[64,128,128]{2,1,0:T(8,128)}) while((s32[]{:T(128)}, f32[4,260,2,8,128]{4,3,2,1,0:T(8,128)}, f32[4,260,2,8,128]{4,3,2,1,0:T(8,128)}, s32[4,260]{1,0:T(4,128)S(1)}, ...), condition=%wide.region_6.7_spmd.clone, body=%wide.region_5.6_spmd.sunk.clone | while | flops 817891072 | bytes 55387264 | solution.py:99
  206.7 76.5 %all-to-all-done.2 = f32[4,260,2,8,128]{4,3,2,1,0:T(8,128)} async-done(((f32[4,260,2,8,128]{4,3,2,1,0:T(8,128)}), f32[4,260,2,8,128]{4,3,2,1,0:T(8,128)}, u32[]{:S(2)}, u32[]{:S(2)}) %all-to-all-start.2) | async-done | bytes 8519712 | tf_op jit(solution)/shard_map/all_to_all | solution.py:100
  295.3 283.1 %while.54 = (s32[]{:T(128)}, f32[9,128,8,8]{1,3,2,0:T(8,128)S(1)}, f32[128,65,128]{2,0,1:T(8,128)}, f32[128,65,2,128]{3,0,1,2:T(8,128)}, s32[128,2]{0,1:T(2,128)...) while((s32[]{:T(128)}, f32[9,128,8,8]{1,3,2,0:T(8,128)S(1)}, ...), condition=%wide.region_8.9_spmd.clone.clone, body=%wide.region_7.8_spmd.clone.sunk.clone | while | flops 1663609216 | bytes 68392240 | solution.py:115
  297.9 19.7 %multiply_add_fusion.8 = (f32[128,65,1,128]{3,0,1,2:T(8,128)S(1)}, f32[128,65,1,128]{3,0,1,2:T(8,128)S(1)}) fusion(f32[128,65,2,128]{3,0,1,2:T(8,128)} %get-tuple-element.828, s32[128]{0:T(128)S(1)} %get-tuple-element.740, s32[65,128]{1,0:T(8,128)S(1)} %get-tuple-element.741, s32[128]{0:T(128)S(1)} %get-tuple-element.742, ...), kind=kLoop, calls=%fused_computation.24.clone.1.clone | loop fusion | flops 23429120 | bytes 17106944 | tf_op jit(solution)/shard_map/while/body/eval_jaxpr/add | solution.py:35
  329.4 19.7 %multiply_add_fusion.8 = (f32[128,65,1,128]{3,0,1,2:T(8,128)S(1)}, f32[128,65,1,128]{3,0,1,2:T(8,128)S(1)}) fusion(f32[128,65,2,128]{3,0,1,2:T(8,128)} %get-tuple-element.828, s32[128]{0:T(128)S(1)} %get-tuple-element.740, s32[65,128]{1,0:T(8,128)S(1)} %get-tuple-element.741, s32[128]{0:T(128)S(1)} %get-tuple-element.742, ...), kind=kLoop, calls=%fused_computation.24.clone.1.clone | loop fusion | flops 23429120 | bytes 17106944 | tf_op jit(solution)/shard_map/while/body/eval_jaxpr/add | solution.py:35
  360.8 19.7 %multiply_add_fusion.8 = (f32[128,65,1,128]{3,0,1,2:T(8,128)S(1)}, f32[128,65,1,128]{3,0,1,2:T(8,128)S(1)}) fusion(f32[128,65,2,128]{3,0,1,2:T(8,128)} %get-tuple-element.828, s32[128]{0:T(128)S(1)} %get-tuple-element.740, s32[65,128]{1,0:T(8,128)S(1)} %get-tuple-element.741, s32[128]{0:T(128)S(1)} %get-tuple-element.742, ...), kind=kLoop, calls=%fused_computation.24.clone.1.clone | loop fusion | flops 23429120 | bytes 17106944 | tf_op jit(solution)/shard_map/while/body/eval_jaxpr/add | solution.py:35
  392.3 19.7 %multiply_add_fusion.8 = (f32[128,65,1,128]{3,0,1,2:T(8,128)S(1)}, f32[128,65,1,128]{3,0,1,2:T(8,128)S(1)}) fusion(f32[128,65,2,128]{3,0,1,2:T(8,128)} %get-tuple-element.828, s32[128]{0:T(128)S(1)} %get-tuple-element.740, s32[65,128]{1,0:T(8,128)S(1)} %get-tuple-element.741, s32[128]{0:T(128)S(1)} %get-tuple-element.742, ...), kind=kLoop, calls=%fused_computation.24.clone.1.clone | loop fusion | flops 23429120 | bytes 17106944 | tf_op jit(solution)/shard_map/while/body/eval_jaxpr/add | solution.py:35
  423.7 19.7 %multiply_add_fusion.8 = (f32[128,65,1,128]{3,0,1,2:T(8,128)S(1)}, f32[128,65,1,128]{3,0,1,2:T(8,128)S(1)}) fusion(f32[128,65,2,128]{3,0,1,2:T(8,128)} %get-tuple-element.828, s32[128]{0:T(128)S(1)} %get-tuple-element.740, s32[65,128]{1,0:T(8,128)S(1)} %get-tuple-element.741, s32[128]{0:T(128)S(1)} %get-tuple-element.742, ...), kind=kLoop, calls=%fused_computation.24.clone.1.clone | loop fusion | flops 23429120 | bytes 17106944 | tf_op jit(solution)/shard_map/while/body/eval_jaxpr/add | solution.py:35
  455.1 19.7 %multiply_add_fusion.8 = (f32[128,65,1,128]{3,0,1,2:T(8,128)S(1)}, f32[128,65,1,128]{3,0,1,2:T(8,128)S(1)}) fusion(f32[128,65,2,128]{3,0,1,2:T(8,128)} %get-tuple-element.828, s32[128]{0:T(128)S(1)} %get-tuple-element.740, s32[65,128]{1,0:T(8,128)S(1)} %get-tuple-element.741, s32[128]{0:T(128)S(1)} %get-tuple-element.742, ...), kind=kLoop, calls=%fused_computation.24.clone.1.clone | loop fusion | flops 23429120 | bytes 17106944 | tf_op jit(solution)/shard_map/while/body/eval_jaxpr/add | solution.py:35
  486.6 19.7 %multiply_add_fusion.8 = (f32[128,65,1,128]{3,0,1,2:T(8,128)S(1)}, f32[128,65,1,128]{3,0,1,2:T(8,128)S(1)}) fusion(f32[128,65,2,128]{3,0,1,2:T(8,128)} %get-tuple-element.828, s32[128]{0:T(128)S(1)} %get-tuple-element.740, s32[65,128]{1,0:T(8,128)S(1)} %get-tuple-element.741, s32[128]{0:T(128)S(1)} %get-tuple-element.742, ...), kind=kLoop, calls=%fused_computation.24.clone.1.clone | loop fusion | flops 23429120 | bytes 17106944 | tf_op jit(solution)/shard_map/while/body/eval_jaxpr/add | solution.py:35
  518.0 19.7 %multiply_add_fusion.8 = (f32[128,65,1,128]{3,0,1,2:T(8,128)S(1)}, f32[128,65,1,128]{3,0,1,2:T(8,128)S(1)}) fusion(f32[128,65,2,128]{3,0,1,2:T(8,128)} %get-tuple-element.828, s32[128]{0:T(128)S(1)} %get-tuple-element.740, s32[65,128]{1,0:T(8,128)S(1)} %get-tuple-element.741, s32[128]{0:T(128)S(1)} %get-tuple-element.742, ...), kind=kLoop, calls=%fused_computation.24.clone.1.clone | loop fusion | flops 23429120 | bytes 17106944 | tf_op jit(solution)/shard_map/while/body/eval_jaxpr/add | solution.py:35
  585.3 40.4 %pmax.7 = f32[128]{0:T(128)S(1)} all-reduce(f32[128]{0:T(128)S(1)} %fusion.84), channel_id=1, replica_groups=mesh['vol'=4,'orient'=4,'dp'=2] {'vol','orient'}, use_global_device_ids=true, to_apply=%region_11.12 | all-reduce | flops 128 | bytes 1024 | tf_op jit(solution)/shard_map/pmax | solution.py:123
  625.8 36.7 %psum.7 = f32[128,8]{0,1:T(8,128)S(1)} all-reduce(f32[128,8]{0,1:T(8,128)S(1)} %fusion.83), channel_id=1, replica_groups=mesh['vol'=4,'orient'=4,'dp'=2] {'vol','orient'}, use_global_device_ids=true, to_apply=%region_13.14 | all-reduce | flops 1024 | bytes 8192 | tf_op jit(solution)/shard_map/psum | solution.py:125
  663.2 299.8 %while.55 = (s32[]{:T(128)}, f32[8,65,2,8,128]{4,0,3,2,1:T(8,128)}, f32[128,65,128]{2,0,1:T(8,128)}, f32[128,65,2,128]{3,0,2,1:T(8,128)}, s32[128,2]{0,1:T(2,128...) while((s32[]{:T(128)}, f32[8,65,2,8,128]{4,0,3,2,1:T(8,128)}, ...), condition=%wide.region_16.17_spmd.clone.clone, body=%wide.region_15.16_spmd.clone.sunk.clone | while | flops 1665739136 | bytes 38507784 | solution.py:141
  665.5 20.7 %multiply_add_fusion.9 = (f32[128,65,1,128]{3,0,2,1:T(8,128)}, f32[128,65,1,128]{3,0,2,1:T(8,128)}) fusion(f32[128,65,2,128]{3,0,2,1:T(8,128)} %get-tuple-element.855, s32[128]{0:T(128)S(1)} %get-tuple-element.771, s32[65,128]{1,0:T(8,128)S(1)} %get-tuple-element.772, s32[128]{0:T(128)S(1)} %get-tuple-element.773, ...), kind=kLoop, calls=%fused_computation.56.clone.1.clone | loop fusion | flops 23429120 | bytes 17106944 | tf_op jit(solution)/shard_map/while/body/eval_jaxpr/add | solution.py:35
  698.3 20.7 %multiply_add_fusion.9 = (f32[128,65,1,128]{3,0,2,1:T(8,128)}, f32[128,65,1,128]{3,0,2,1:T(8,128)}) fusion(f32[128,65,2,128]{3,0,2,1:T(8,128)} %get-tuple-element.855, s32[128]{0:T(128)S(1)} %get-tuple-element.771, s32[65,128]{1,0:T(8,128)S(1)} %get-tuple-element.772, s32[128]{0:T(128)S(1)} %get-tuple-element.773, ...), kind=kLoop, calls=%fused_computation.56.clone.1.clone | loop fusion | flops 23429120 | bytes 17106944 | tf_op jit(solution)/shard_map/while/body/eval_jaxpr/add | solution.py:35
  731.7 20.7 %multiply_add_fusion.9 = (f32[128,65,1,128]{3,0,2,1:T(8,128)}, f32[128,65,1,128]{3,0,2,1:T(8,128)}) fusion(f32[128,65,2,128]{3,0,2,1:T(8,128)} %get-tuple-element.855, s32[128]{0:T(128)S(1)} %get-tuple-element.771, s32[65,128]{1,0:T(8,128)S(1)} %get-tuple-element.772, s32[128]{0:T(128)S(1)} %get-tuple-element.773, ...), kind=kLoop, calls=%fused_computation.56.clone.1.clone | loop fusion | flops 23429120 | bytes 17106944 | tf_op jit(solution)/shard_map/while/body/eval_jaxpr/add | solution.py:35
  765.1 20.7 %multiply_add_fusion.9 = (f32[128,65,1,128]{3,0,2,1:T(8,128)}, f32[128,65,1,128]{3,0,2,1:T(8,128)}) fusion(f32[128,65,2,128]{3,0,2,1:T(8,128)} %get-tuple-element.855, s32[128]{0:T(128)S(1)} %get-tuple-element.771, s32[65,128]{1,0:T(8,128)S(1)} %get-tuple-element.772, s32[128]{0:T(128)S(1)} %get-tuple-element.773, ...), kind=kLoop, calls=%fused_computation.56.clone.1.clone | loop fusion | flops 23429120 | bytes 17106944 | tf_op jit(solution)/shard_map/while/body/eval_jaxpr/add | solution.py:35
  798.4 20.7 %multiply_add_fusion.9 = (f32[128,65,1,128]{3,0,2,1:T(8,128)}, f32[128,65,1,128]{3,0,2,1:T(8,128)}) fusion(f32[128,65,2,128]{3,0,2,1:T(8,128)} %get-tuple-element.855, s32[128]{0:T(128)S(1)} %get-tuple-element.771, s32[65,128]{1,0:T(8,128)S(1)} %get-tuple-element.772, s32[128]{0:T(128)S(1)} %get-tuple-element.773, ...), kind=kLoop, calls=%fused_computation.56.clone.1.clone | loop fusion | flops 23429120 | bytes 17106944 | tf_op jit(solution)/shard_map/while/body/eval_jaxpr/add | solution.py:35
  831.8 20.7 %multiply_add_fusion.9 = (f32[128,65,1,128]{3,0,2,1:T(8,128)}, f32[128,65,1,128]{3,0,2,1:T(8,128)}) fusion(f32[128,65,2,128]{3,0,2,1:T(8,128)} %get-tuple-element.855, s32[128]{0:T(128)S(1)} %get-tuple-element.771, s32[65,128]{1,0:T(8,128)S(1)} %get-tuple-element.772, s32[128]{0:T(128)S(1)} %get-tuple-element.773, ...), kind=kLoop, calls=%fused_computation.56.clone.1.clone | loop fusion | flops 23429120 | bytes 17106944 | tf_op jit(solution)/shard_map/while/body/eval_jaxpr/add | solution.py:35
  865.2 20.7 %multiply_add_fusion.9 = (f32[128,65,1,128]{3,0,2,1:T(8,128)}, f32[128,65,1,128]{3,0,2,1:T(8,128)}) fusion(f32[128,65,2,128]{3,0,2,1:T(8,128)} %get-tuple-element.855, s32[128]{0:T(128)S(1)} %get-tuple-element.771, s32[65,128]{1,0:T(8,128)S(1)} %get-tuple-element.772, s32[128]{0:T(128)S(1)} %get-tuple-element.773, ...), kind=kLoop, calls=%fused_computation.56.clone.1.clone | loop fusion | flops 23429120 | bytes 17106944 | tf_op jit(solution)/shard_map/while/body/eval_jaxpr/add | solution.py:35
  898.6 20.7 %multiply_add_fusion.9 = (f32[128,65,1,128]{3,0,2,1:T(8,128)}, f32[128,65,1,128]{3,0,2,1:T(8,128)}) fusion(f32[128,65,2,128]{3,0,2,1:T(8,128)} %get-tuple-element.855, s32[128]{0:T(128)S(1)} %get-tuple-element.771, s32[65,128]{1,0:T(8,128)S(1)} %get-tuple-element.772, s32[128]{0:T(128)S(1)} %get-tuple-element.773, ...), kind=kLoop, calls=%fused_computation.56.clone.1.clone | loop fusion | flops 23429120 | bytes 17106944 | tf_op jit(solution)/shard_map/while/body/eval_jaxpr/add | solution.py:35
  932.0 20.7 %multiply_add_fusion.9 = (f32[128,65,1,128]{3,0,2,1:T(8,128)}, f32[128,65,1,128]{3,0,2,1:T(8,128)}) fusion(f32[128,65,2,128]{3,0,2,1:T(8,128)} %get-tuple-element.855, s32[128]{0:T(128)S(1)} %get-tuple-element.771, s32[65,128]{1,0:T(8,128)S(1)} %get-tuple-element.772, s32[128]{0:T(128)S(1)} %get-tuple-element.773, ...), kind=kLoop, calls=%fused_computation.56.clone.1.clone | loop fusion | flops 23429120 | bytes 17106944 | tf_op jit(solution)/shard_map/while/body/eval_jaxpr/add | solution.py:35
  977.5 69.6 %scatter_fusion = f32[1040,3,8,128]{3,2,1,0:T(8,128)} fusion(f32[1040,3,8,128]{3,2,1,0:T(8,128)} %broadcast_in_dim.61, s32[520]{0:T(1024)S(1)} %fusion.92, f32[520,3,8,128]{3,2,1,0:T(8,128)} %pad_maximum_fusion), kind=kCustom, calls=%fused_computation.6 | custom fusion | bytes 19171360 | tf_op jit(solution)/shard_map/scatter | solution.py:147
  1053.5 124.3 %all-to-all-done.3 = f32[4,260,3,8,128]{4,3,2,1,0:T(8,128)} async-done(((f32[4,260,3,8,128]{4,3,2,1,0:T(8,128)}), f32[4,260,3,8,128]{4,3,2,1,0:T(8,128)}, u32[]{:S(2)}, u32[]{:S(2)}) %all-to-all-start.3) | async-done | bytes 12779552 | tf_op jit(solution)/shard_map/all_to_all | solution.py:151
  1177.8 182.0 %while.53 = (s32[]{:T(128)}, f32[4,260,3,8,128]{4,3,2,1,0:T(8,128)}, f32[4,260,3,8,128]{4,3,2,1,0:T(8,128)}, s32[4,260]{1,0:T(4,128)}, f32[64,128,128]{2,1,0:T(8,128)}) while((s32[]{:T(128)}, f32[4,260,3,8,128]{4,3,2,1,0:T(8,128)}, f32[4,260,3,8,128]{4,3,2,1,0:T(8,128)}, s32[4,260]{1,0:T(4,128)}, ...), condition=%wide.region_20.21_spmd.clone, body=%wide.region_19.20_spmd.sunk.clone | while | flops 1226835712 | bytes 57517184 | solution.py:152
  1193.3 30.2 %bitcast_dynamic-update-slice_fusion.7 = f32[4,260,3,8,128]{4,3,2,1,0:T(8,128)} fusion(f32[4,260,3,8,128]{4,3,2,1,0:T(8,128)} %get-tuple-element.867, s32[]{:T(128)} %get-tuple-element.866, f32[260,128,128]{2,1,0:T(8,128)} %gather_fusion.1, f32[4,260,3,8,128]{4,3,2,1,0:T(8,128)} %get-tuple-element.873), kind=kOutput, calls=%fused_computation.87.clone.1.clone | convolution fusion | flops 1226833920 | bytes 23430144 | tf_op jit(solution)/shard_map/while/body/eval_jaxpr/nmkq,nrq->nmkr/dot_general | solution.py:47
  1238.9 30.2 %bitcast_dynamic-update-slice_fusion.7 = f32[4,260,3,8,128]{4,3,2,1,0:T(8,128)} fusion(f32[4,260,3,8,128]{4,3,2,1,0:T(8,128)} %get-tuple-element.867, s32[]{:T(128)} %get-tuple-element.866, f32[260,128,128]{2,1,0:T(8,128)} %gather_fusion.1, f32[4,260,3,8,128]{4,3,2,1,0:T(8,128)} %get-tuple-element.873), kind=kOutput, calls=%fused_computation.87.clone.1.clone | convolution fusion | flops 1226833920 | bytes 23430144 | tf_op jit(solution)/shard_map/while/body/eval_jaxpr/nmkq,nrq->nmkr/dot_general | solution.py:47
  1284.2 30.2 %bitcast_dynamic-update-slice_fusion.7 = f32[4,260,3,8,128]{4,3,2,1,0:T(8,128)} fusion(f32[4,260,3,8,128]{4,3,2,1,0:T(8,128)} %get-tuple-element.867, s32[]{:T(128)} %get-tuple-element.866, f32[260,128,128]{2,1,0:T(8,128)} %gather_fusion.1, f32[4,260,3,8,128]{4,3,2,1,0:T(8,128)} %get-tuple-element.873), kind=kOutput, calls=%fused_computation.87.clone.1.clone | convolution fusion | flops 1226833920 | bytes 23430144 | tf_op jit(solution)/shard_map/while/body/eval_jaxpr/nmkq,nrq->nmkr/dot_general | solution.py:47
  1329.5 30.2 %bitcast_dynamic-update-slice_fusion.7 = f32[4,260,3,8,128]{4,3,2,1,0:T(8,128)} fusion(f32[4,260,3,8,128]{4,3,2,1,0:T(8,128)} %get-tuple-element.867, s32[]{:T(128)} %get-tuple-element.866, f32[260,128,128]{2,1,0:T(8,128)} %gather_fusion.1, f32[4,260,3,8,128]{4,3,2,1,0:T(8,128)} %get-tuple-element.873), kind=kOutput, calls=%fused_computation.87.clone.1.clone | convolution fusion | flops 1226833920 | bytes 23430144 | tf_op jit(solution)/shard_map/while/body/eval_jaxpr/nmkq,nrq->nmkr/dot_general | solution.py:47
  1368.4 144.0 %scatter_fusion.1 = f32[2080,3,8,128]{3,2,1,0:T(8,128)} fusion(f32[2080,3,8,128]{3,2,1,0:T(8,128)} %broadcast_in_dim.53, s32[1040]{0:T(1024)S(1)} %copy-done.7, f32[1040,3,8,128]{3,2,1,0:T(8,128)} %bitcast.202), kind=kCustom, calls=%fused_computation.7 | custom fusion | flops 3194880 | bytes 38342720 | tf_op jit(solution)/shard_map/scatter-add | solution.py:155
  1513.7 248.7 %reduce-scatter.2.cloned.1.call-done = f32[4,65,3,8,128]{4,3,2,1,0:T(8,128)} async-done(((f32[32,65,3,8,128]{4,3,2,1,0:T(8,128)}), f32[4,65,3,8,128]{4,3,2,1,0:T(8,128)}) %reduce-scatter.2.cloned.1.call-update) | async-done | bytes 3194896 | tf_op jit(solution)/shard_map/reduce_scatter | solution.py:157
  (244 shorter events, 516.3 us)
Async XLA Ops:
  16.5 10.7 all-to-all-start
  27.2 25.3 %all-to-all-start.1 = ((s32[4,1,260]{2,1,0:T(1,128)}), s32[4,1,260]{2,1,0:T(1,128)S(1)}, u32[]{:S(2)}, u32[]{:S(2)}) async-start(s32[4,1,260]{2,1,0:T(1,128)} %all_to_all.22), calls=%async_computation.1 | async-start | bytes 12288 | tf_op jit(solution)/shard_map/all_to_all | solution.py:94
  31.7 13.2 copy-start.6
  182.7 100.4 %all-to-all-start.2 = ((f32[4,260,2,8,128]{4,3,2,1,0:T(8,128)}), f32[4,260,2,8,128]{4,3,2,1,0:T(8,128)}, u32[]{:S(2)}, u32[]{:S(2)}) async-start(f32[4,260,2,8,128]{4,3,2,1,0:T(8,128)} %get-tuple-element.363), calls=%async_computation.2 | async-start | bytes 17039360 | tf_op jit(solution)/shard_map/all_to_all | solution.py:100
  188.8 8.1 slice-start
  188.8 8.1 slice-start.1
  188.8 8.1 slice-start.2
  196.9 4.6 copy-start.13
  196.9 4.6 copy-start.14
  196.9 4.6 copy-start.8
  289.6 3.5 copy-start.3
  297.9 19.7 %copy-start.1 = (f32[128,65,128]{2,0,1:T(8,128)S(1)}, f32[128,65,128]{2,0,1:T(8,128)}, u32[]{:S(2)}) copy-start(f32[128,65,128]{2,0,1:T(8,128)} %get-tuple-element.827) | copy-start | bytes 12779524 | tf_op jit(solution)/shard_map/while
  297.9 19.7 %copy-start.2 = (f32[8,65,2,8,128]{4,3,1,0,2:T(8,128)S(1)}, f32[8,65,2,8,128]{4,3,1,0,2:T(8,128)}, u32[]{:S(2)}) copy-start(f32[8,65,2,8,128]{4,3,1,0,2:T(8,128)} %get-tuple-element.831) | copy-start | bytes 12779524 | tf_op jit(solution)/shard_map/while
  329.4 19.7 %copy-start.1 = (f32[128,65,128]{2,0,1:T(8,128)S(1)}, f32[128,65,128]{2,0,1:T(8,128)}, u32[]{:S(2)}) copy-start(f32[128,65,128]{2,0,1:T(8,128)} %get-tuple-element.827) | copy-start | bytes 12779524 | tf_op jit(solution)/shard_map/while
  329.4 19.7 %copy-start.2 = (f32[8,65,2,8,128]{4,3,1,0,2:T(8,128)S(1)}, f32[8,65,2,8,128]{4,3,1,0,2:T(8,128)}, u32[]{:S(2)}) copy-start(f32[8,65,2,8,128]{4,3,1,0,2:T(8,128)} %get-tuple-element.831) | copy-start | bytes 12779524 | tf_op jit(solution)/shard_map/while
  360.8 19.7 %copy-start.1 = (f32[128,65,128]{2,0,1:T(8,128)S(1)}, f32[128,65,128]{2,0,1:T(8,128)}, u32[]{:S(2)}) copy-start(f32[128,65,128]{2,0,1:T(8,128)} %get-tuple-element.827) | copy-start | bytes 12779524 | tf_op jit(solution)/shard_map/while
  360.8 19.7 %copy-start.2 = (f32[8,65,2,8,128]{4,3,1,0,2:T(8,128)S(1)}, f32[8,65,2,8,128]{4,3,1,0,2:T(8,128)}, u32[]{:S(2)}) copy-start(f32[8,65,2,8,128]{4,3,1,0,2:T(8,128)} %get-tuple-element.831) | copy-start | bytes 12779524 | tf_op jit(solution)/shard_map/while
  392.2 19.7 %copy-start.1 = (f32[128,65,128]{2,0,1:T(8,128)S(1)}, f32[128,65,128]{2,0,1:T(8,128)}, u32[]{:S(2)}) copy-start(f32[128,65,128]{2,0,1:T(8,128)} %get-tuple-element.827) | copy-start | bytes 12779524 | tf_op jit(solution)/shard_map/while
  392.2 19.7 %copy-start.2 = (f32[8,65,2,8,128]{4,3,1,0,2:T(8,128)S(1)}, f32[8,65,2,8,128]{4,3,1,0,2:T(8,128)}, u32[]{:S(2)}) copy-start(f32[8,65,2,8,128]{4,3,1,0,2:T(8,128)} %get-tuple-element.831) | copy-start | bytes 12779524 | tf_op jit(solution)/shard_map/while
  423.7 19.7 %copy-start.1 = (f32[128,65,128]{2,0,1:T(8,128)S(1)}, f32[128,65,128]{2,0,1:T(8,128)}, u32[]{:S(2)}) copy-start(f32[128,65,128]{2,0,1:T(8,128)} %get-tuple-element.827) | copy-start | bytes 12779524 | tf_op jit(solution)/shard_map/while
  423.7 19.7 %copy-start.2 = (f32[8,65,2,8,128]{4,3,1,0,2:T(8,128)S(1)}, f32[8,65,2,8,128]{4,3,1,0,2:T(8,128)}, u32[]{:S(2)}) copy-start(f32[8,65,2,8,128]{4,3,1,0,2:T(8,128)} %get-tuple-element.831) | copy-start | bytes 12779524 | tf_op jit(solution)/shard_map/while
  455.1 19.7 %copy-start.1 = (f32[128,65,128]{2,0,1:T(8,128)S(1)}, f32[128,65,128]{2,0,1:T(8,128)}, u32[]{:S(2)}) copy-start(f32[128,65,128]{2,0,1:T(8,128)} %get-tuple-element.827) | copy-start | bytes 12779524 | tf_op jit(solution)/shard_map/while
  455.1 19.7 %copy-start.2 = (f32[8,65,2,8,128]{4,3,1,0,2:T(8,128)S(1)}, f32[8,65,2,8,128]{4,3,1,0,2:T(8,128)}, u32[]{:S(2)}) copy-start(f32[8,65,2,8,128]{4,3,1,0,2:T(8,128)} %get-tuple-element.831) | copy-start | bytes 12779524 | tf_op jit(solution)/shard_map/while
  486.6 19.7 %copy-start.1 = (f32[128,65,128]{2,0,1:T(8,128)S(1)}, f32[128,65,128]{2,0,1:T(8,128)}, u32[]{:S(2)}) copy-start(f32[128,65,128]{2,0,1:T(8,128)} %get-tuple-element.827) | copy-start | bytes 12779524 | tf_op jit(solution)/shard_map/while
  486.6 19.7 %copy-start.2 = (f32[8,65,2,8,128]{4,3,1,0,2:T(8,128)S(1)}, f32[8,65,2,8,128]{4,3,1,0,2:T(8,128)}, u32[]{:S(2)}) copy-start(f32[8,65,2,8,128]{4,3,1,0,2:T(8,128)} %get-tuple-element.831) | copy-start | bytes 12779524 | tf_op jit(solution)/shard_map/while
  518.0 19.7 %copy-start.1 = (f32[128,65,128]{2,0,1:T(8,128)S(1)}, f32[128,65,128]{2,0,1:T(8,128)}, u32[]{:S(2)}) copy-start(f32[128,65,128]{2,0,1:T(8,128)} %get-tuple-element.827) | copy-start | bytes 12779524 | tf_op jit(solution)/shard_map/while
  518.0 19.7 %copy-start.2 = (f32[8,65,2,8,128]{4,3,1,0,2:T(8,128)S(1)}, f32[8,65,2,8,128]{4,3,1,0,2:T(8,128)}, u32[]{:S(2)}) copy-start(f32[8,65,2,8,128]{4,3,1,0,2:T(8,128)} %get-tuple-element.831) | copy-start | bytes 12779524 | tf_op jit(solution)/shard_map/while
  549.4 19.7 %copy-start.1 = (f32[128,65,128]{2,0,1:T(8,128)S(1)}, f32[128,65,128]{2,0,1:T(8,128)}, u32[]{:S(2)}) copy-start(f32[128,65,128]{2,0,1:T(8,128)} %get-tuple-element.827) | copy-start | bytes 12779524 | tf_op jit(solution)/shard_map/while
  549.5 19.7 %copy-start.2 = (f32[8,65,2,8,128]{4,3,1,0,2:T(8,128)S(1)}, f32[8,65,2,8,128]{4,3,1,0,2:T(8,128)}, u32[]{:S(2)}) copy-start(f32[8,65,2,8,128]{4,3,1,0,2:T(8,128)} %get-tuple-element.831) | copy-start | bytes 12779524 | tf_op jit(solution)/shard_map/while
  1047.1 130.7 %all-to-all-start.3 = ((f32[4,260,3,8,128]{4,3,2,1,0:T(8,128)}), f32[4,260,3,8,128]{4,3,2,1,0:T(8,128)}, u32[]{:S(2)}, u32[]{:S(2)}) async-start(f32[4,260,3,8,128]{4,3,2,1,0:T(8,128)} %bitcast.196), calls=%async_computation.3 | async-start | bytes 25559040 | tf_op jit(solution)/shard_map/all_to_all | solution.py:151
  1053.4 709.0 %reduce-scatter.2.cloned.1.call-start = ((), (), s32[]{:S(2)}) async-start(), calls=%async_computation.5 | async-start | bytes 28753920 | tf_op jit(solution)/shard_map/reduce_scatter | solution.py:157
  1359.7 8.7 copy-start.7
  (7 other events, 8.9 us)
Sparse Core Ops, SparseCore 0:
  1512.6 249.7 reduce-scatter.1
where the time goes:
time: 1780 us; the launch traced here: 1770 us
  other arithmetic  535 us (30%)
  waiting for transfers between devices  449 us (25%)
  matrix products  376 us (21%)
  local copies, waits for them, and re-layouts  261 us (15%)
  blocking collectives  77.1 us (4%)
  loops' own time  34 us (2%)
  starting transfers between devices  22 us (1%)
    add x18, other arithmetic, moved_images(): real_part * cosine + imag_part * sine_part  363 us
    reduce_scatter x1, waiting for transfers between devices, shards(): lax.psum_scatter(accumulated, ('orient', 'dp'), scatter_dimension=0, tile...  249 us
    scatter-add x1, other arithmetic, shards(): accumulated.at[cell_index]  144 us
    all_to_all x1, waiting for transfers between devices, shards(): lax.all_to_all(outgoing, 'vol', split_axis=0, concat_axis=0, tiled=True)  124 us
    dot_general x4, matrix products, back_project(): return jnp.einsum('nmkq,nrq->nmkr', tile_rows, matrices, precision=PRECISE)  121 us
    dot_general x9, matrix products, add_step(): jnp.einsum('ikp,itcq->ptckq', share_step, ctf[:, :, None, :] * moved, pre...  92.9 us
    dot_general x9, matrix products, score_step(): jnp.einsum('itcq,ptckq->ikp', ctf_noise[:, :, None, :] * moved, slices, p...  81.5 us
    all_to_all x1, waiting for transfers between devices, shards(): lax.all_to_all(pieces, 'vol', split_axis=0, concat_axis=0, tiled=True)  76.5 us
  transfers between devices with their start and end apart: 5, of which 3 were waited for; matrix products, arithmetic and copies ran while one was open for 2% of the time, Pallas kernels for 0%

commit v1 on v0

--- a/solution.py
+++ b/solution.py
@@ -122,7 +122,7 @@
     scores = 2.0 * cross_term - norm_term[None] + earlier_class_term[None, :, :, None]
     peak_value = lax.pmax(jnp.max(scores, axis=(0, 2, 3)), ("vol", "orient"))
     exp_scores = jnp.exp(scores - peak_value[None, :, None, None])
-    class_mass = lax.psum(jnp.sum(exp_scores, axis=(0, 3)), ("vol", "orient"))
+    class_mass = lax.psum(lax.psum(jnp.sum(exp_scores, axis=(0, 3)), "orient"), "vol")
     mass_total = jnp.sum(class_mass, axis=1)
     posterior = class_mass / mass_total[:, None]
     evidence = peak_value + jnp.log(mass_total)

time: 1780 us -> 1760 us (0.989)
  blocking collectives: 77.1 us -> 57.5 us
    psum x1 -> x2, blocking collectives: 36.7 us -> 17.1 us  [the longest x1 8.76 us: shards(): lax.psum(lax.psum(jnp.sum(exp_scores, axis=(0, 3)), 'orient'), 'vol')]
  transfers between devices with their start and end apart: 5 -> 5, of which waited for: 3 -> 3; matrix products, arithmetic and copies ran while one was open for 2% -> 3% of each run, Pallas kernels for 0% -> 0%
where the time goes in v1:
time: 1760 us; the launch traced here: 1750 us
  other arithmetic  535 us (30%)
  waiting for transfers between devices  452 us (26%)
  matrix products  376 us (21%)
  local copies, waits for them, and re-layouts  261 us (15%)
  blocking collectives  57.5 us (3%)
  loops' own time  34 us (2%)
  starting transfers between devices  22 us (1%)
    add x18, other arithmetic, moved_images(): real_part * cosine + imag_part * sine_part  363 us
    reduce_scatter x1, waiting for transfers between devices, shards(): lax.psum_scatter(accumulated, ('orient', 'dp'), scatter_dimension=0, tile...  249 us
    scatter-add x1, other arithmetic, shards(): accumulated.at[cell_index]  144 us
    all_to_all x1, waiting for transfers between devices, shards(): lax.all_to_all(outgoing, 'vol', split_axis=0, concat_axis=0, tiled=True)  127 us
    dot_general x4, matrix products, back_project(): return jnp.einsum('nmkq,nrq->nmkr', tile_rows, matrices, precision=PRECISE)  121 us
    dot_general x9, matrix products, add_step(): jnp.einsum('ikp,itcq->ptckq', share_step, ctf[:, :, None, :] * moved, pre...  92.9 us
    dot_general x9, matrix products, score_step(): jnp.einsum('itcq,ptckq->ikp', ctf_noise[:, :, None, :] * moved, slices, p...  81.5 us
    all_to_all x1, waiting for transfers between devices, shards(): lax.all_to_all(pieces, 'vol', split_axis=0, concat_axis=0, tiled=True)  76.5 us
  transfers between devices with their start and end apart: 5, of which 3 were waited for; matrix products, arithmetic and copies ran while one was open for 3% of the time, Pallas kernels for 0%

profile of v1, /device:TPU:0, one launch (start us, length us, event | category | flops | bytes accessed | tf_op | source)
XLA Modules:
  0.0 1752.4 jit_solution(3877906259512375141)
XLA Ops:
  52.4 129.7 %while.52 = (s32[]{:T(128)}, f32[4,260,2,8,128]{4,3,2,1,0:T(8,128)}, f32[4,260,2,8,128]{4,3,2,1,0:T(8,128)}, s32[4,260]{1,0:T(4,128)S(1)}, f32[64,128,128]{2,1,0:T(8,128)}) while((s32[]{:T(128)}, f32[4,260,2,8,128]{4,3,2,1,0:T(8,128)}, f32[4,260,2,8,128]{4,3,2,1,0:T(8,128)}, s32[4,260]{1,0:T(4,128)S(1)}, ...), condition=%wide.region_6.7_spmd.clone, body=%wide.region_5.6_spmd.sunk.clone | while | flops 817891072 | bytes 55387264 | solution.py:99
  206.7 76.5 %all-to-all-done.2 = f32[4,260,2,8,128]{4,3,2,1,0:T(8,128)} async-done(((f32[4,260,2,8,128]{4,3,2,1,0:T(8,128)}), f32[4,260,2,8,128]{4,3,2,1,0:T(8,128)}, u32[]{:S(2)}, u32[]{:S(2)}) %all-to-all-start.2) | async-done | bytes 8519712 | tf_op jit(solution)/shard_map/all_to_all | solution.py:100
  295.3 283.1 %while.54 = (s32[]{:T(128)}, f32[9,128,8,8]{1,3,2,0:T(8,128)S(1)}, f32[128,65,128]{2,0,1:T(8,128)}, f32[128,65,2,128]{3,0,1,2:T(8,128)}, s32[128,2]{0,1:T(2,128)...) while((s32[]{:T(128)}, f32[9,128,8,8]{1,3,2,0:T(8,128)S(1)}, ...), condition=%wide.region_8.9_spmd.clone.clone, body=%wide.region_7.8_spmd.clone.sunk.clone | while | flops 1663609216 | bytes 68392240 | solution.py:115
  297.9 19.7 %multiply_add_fusion.8 = (f32[128,65,1,128]{3,0,1,2:T(8,128)S(1)}, f32[128,65,1,128]{3,0,1,2:T(8,128)S(1)}) fusion(f32[128,65,2,128]{3,0,1,2:T(8,128)} %get-tuple-element.828, s32[128]{0:T(128)S(1)} %get-tuple-element.740, s32[65,128]{1,0:T(8,128)S(1)} %get-tuple-element.741, s32[128]{0:T(128)S(1)} %get-tuple-element.742, ...), kind=kLoop, calls=%fused_computation.24.clone.1.clone | loop fusion | flops 23429120 | bytes 17106944 | tf_op jit(solution)/shard_map/while/body/eval_jaxpr/add | solution.py:35
  329.4 19.7 %multiply_add_fusion.8 = (f32[128,65,1,128]{3,0,1,2:T(8,128)S(1)}, f32[128,65,1,128]{3,0,1,2:T(8,128)S(1)}) fusion(f32[128,65,2,128]{3,0,1,2:T(8,128)} %get-tuple-element.828, s32[128]{0:T(128)S(1)} %get-tuple-element.740, s32[65,128]{1,0:T(8,128)S(1)} %get-tuple-element.741, s32[128]{0:T(128)S(1)} %get-tuple-element.742, ...), kind=kLoop, calls=%fused_computation.24.clone.1.clone | loop fusion | flops 23429120 | bytes 17106944 | tf_op jit(solution)/shard_map/while/body/eval_jaxpr/add | solution.py:35
  360.8 19.7 %multiply_add_fusion.8 = (f32[128,65,1,128]{3,0,1,2:T(8,128)S(1)}, f32[128,65,1,128]{3,0,1,2:T(8,128)S(1)}) fusion(f32[128,65,2,128]{3,0,1,2:T(8,128)} %get-tuple-element.828, s32[128]{0:T(128)S(1)} %get-tuple-element.740, s32[65,128]{1,0:T(8,128)S(1)} %get-tuple-element.741, s32[128]{0:T(128)S(1)} %get-tuple-element.742, ...), kind=kLoop, calls=%fused_computation.24.clone.1.clone | loop fusion | flops 23429120 | bytes 17106944 | tf_op jit(solution)/shard_map/while/body/eval_jaxpr/add | solution.py:35
  392.3 19.7 %multiply_add_fusion.8 = (f32[128,65,1,128]{3,0,1,2:T(8,128)S(1)}, f32[128,65,1,128]{3,0,1,2:T(8,128)S(1)}) fusion(f32[128,65,2,128]{3,0,1,2:T(8,128)} %get-tuple-element.828, s32[128]{0:T(128)S(1)} %get-tuple-element.740, s32[65,128]{1,0:T(8,128)S(1)} %get-tuple-element.741, s32[128]{0:T(128)S(1)} %get-tuple-element.742, ...), kind=kLoop, calls=%fused_computation.24.clone.1.clone | loop fusion | flops 23429120 | bytes 17106944 | tf_op jit(solution)/shard_map/while/body/eval_jaxpr/add | solution.py:35
  423.7 19.7 %multiply_add_fusion.8 = (f32[128,65,1,128]{3,0,1,2:T(8,128)S(1)}, f32[128,65,1,128]{3,0,1,2:T(8,128)S(1)}) fusion(f32[128,65,2,128]{3,0,1,2:T(8,128)} %get-tuple-element.828, s32[128]{0:T(128)S(1)} %get-tuple-element.740, s32[65,128]{1,0:T(8,128)S(1)} %get-tuple-element.741, s32[128]{0:T(128)S(1)} %get-tuple-element.742, ...), kind=kLoop, calls=%fused_computation.24.clone.1.clone | loop fusion | flops 23429120 | bytes 17106944 | tf_op jit(solution)/shard_map/while/body/eval_jaxpr/add | solution.py:35
  455.1 19.7 %multiply_add_fusion.8 = (f32[128,65,1,128]{3,0,1,2:T(8,128)S(1)}, f32[128,65,1,128]{3,0,1,2:T(8,128)S(1)}) fusion(f32[128,65,2,128]{3,0,1,2:T(8,128)} %get-tuple-element.828, s32[128]{0:T(128)S(1)} %get-tuple-element.740, s32[65,128]{1,0:T(8,128)S(1)} %get-tuple-element.741, s32[128]{0:T(128)S(1)} %get-tuple-element.742, ...), kind=kLoop, calls=%fused_computation.24.clone.1.clone | loop fusion | flops 23429120 | bytes 17106944 | tf_op jit(solution)/shard_map/while/body/eval_jaxpr/add | solution.py:35
  486.6 19.7 %multiply_add_fusion.8 = (f32[128,65,1,128]{3,0,1,2:T(8,128)S(1)}, f32[128,65,1,128]{3,0,1,2:T(8,128)S(1)}) fusion(f32[128,65,2,128]{3,0,1,2:T(8,128)} %get-tuple-element.828, s32[128]{0:T(128)S(1)} %get-tuple-element.740, s32[65,128]{1,0:T(8,128)S(1)} %get-tuple-element.741, s32[128]{0:T(128)S(1)} %get-tuple-element.742, ...), kind=kLoop, calls=%fused_computation.24.clone.1.clone | loop fusion | flops 23429120 | bytes 17106944 | tf_op jit(solution)/shard_map/while/body/eval_jaxpr/add | solution.py:35
  518.0 19.7 %multiply_add_fusion.8 = (f32[128,65,1,128]{3,0,1,2:T(8,128)S(1)}, f32[128,65,1,128]{3,0,1,2:T(8,128)S(1)}) fusion(f32[128,65,2,128]{3,0,1,2:T(8,128)} %get-tuple-element.828, s32[128]{0:T(128)S(1)} %get-tuple-element.740, s32[65,128]{1,0:T(8,128)S(1)} %get-tuple-element.741, s32[128]{0:T(128)S(1)} %get-tuple-element.742, ...), kind=kLoop, calls=%fused_computation.24.clone.1.clone | loop fusion | flops 23429120 | bytes 17106944 | tf_op jit(solution)/shard_map/while/body/eval_jaxpr/add | solution.py:35
  549.5 19.7 %multiply_add_fusion.8 = (f32[128,65,1,128]{3,0,1,2:T(8,128)S(1)}, f32[128,65,1,128]{3,0,1,2:T(8,128)S(1)}) fusion(f32[128,65,2,128]{3,0,1,2:T(8,128)} %get-tuple-element.828, s32[128]{0:T(128)S(1)} %get-tuple-element.740, s32[65,128]{1,0:T(8,128)S(1)} %get-tuple-element.741, s32[128]{0:T(128)S(1)} %get-tuple-element.742, ...), kind=kLoop, calls=%fused_computation.24.clone.1.clone | loop fusion | flops 23429120 | bytes 17106944 | tf_op jit(solution)/shard_map/while/body/eval_jaxpr/add | solution.py:35
  585.3 40.4 %pmax.7 = f32[128]{0:T(128)S(1)} all-reduce(f32[128]{0:T(128)S(1)} %fusion.84), channel_id=1, replica_groups=mesh['vol'=4,'orient'=4,'dp'=2] {'vol','orient'}, use_global_device_ids=true, to_apply=%region_11.12 | all-reduce | flops 128 | bytes 1024 | tf_op jit(solution)/shard_map/pmax | solution.py:123
  643.6 299.8 %while.55 = (s32[]{:T(128)}, f32[8,65,2,8,128]{4,0,3,2,1:T(8,128)}, f32[128,65,128]{2,0,1:T(8,128)}, f32[128,65,2,128]{3,0,2,1:T(8,128)}, s32[128,2]{0,1:T(2,128...) while((s32[]{:T(128)}, f32[8,65,2,8,128]{4,0,3,2,1:T(8,128)}, ...), condition=%wide.region_17.18_spmd.clone.clone, body=%wide.region_16.17_spmd.clone.sunk.clone | while | flops 1665739136 | bytes 38507784 | solution.py:141
  645.9 20.7 %multiply_add_fusion.9 = (f32[128,65,1,128]{3,0,2,1:T(8,128)}, f32[128,65,1,128]{3,0,2,1:T(8,128)}) fusion(f32[128,65,2,128]{3,0,2,1:T(8,128)} %get-tuple-element.855, s32[128]{0:T(128)S(1)} %get-tuple-element.771, s32[65,128]{1,0:T(8,128)S(1)} %get-tuple-element.772, s32[128]{0:T(128)S(1)} %get-tuple-element.773, ...), kind=kLoop, calls=%fused_computation.56.clone.1.clone | loop fusion | flops 23429120 | bytes 17106944 | tf_op jit(solution)/shard_map/while/body/eval_jaxpr/add | solution.py:35
  678.7 20.7 %multiply_add_fusion.9 = (f32[128,65,1,128]{3,0,2,1:T(8,128)}, f32[128,65,1,128]{3,0,2,1:T(8,128)}) fusion(f32[128,65,2,128]{3,0,2,1:T(8,128)} %get-tuple-element.855, s32[128]{0:T(128)S(1)} %get-tuple-element.771, s32[65,128]{1,0:T(8,128)S(1)} %get-tuple-element.772, s32[128]{0:T(128)S(1)} %get-tuple-element.773, ...), kind=kLoop, calls=%fused_computation.56.clone.1.clone | loop fusion | flops 23429120 | bytes 17106944 | tf_op jit(solution)/shard_map/while/body/eval_jaxpr/add | solution.py:35
  712.1 20.7 %multiply_add_fusion.9 = (f32[128,65,1,128]{3,0,2,1:T(8,128)}, f32[128,65,1,128]{3,0,2,1:T(8,128)}) fusion(f32[128,65,2,128]{3,0,2,1:T(8,128)} %get-tuple-element.855, s32[128]{0:T(128)S(1)} %get-tuple-element.771, s32[65,128]{1,0:T(8,128)S(1)} %get-tuple-element.772, s32[128]{0:T(128)S(1)} %get-tuple-element.773, ...), kind=kLoop, calls=%fused_computation.56.clone.1.clone | loop fusion | flops 23429120 | bytes 17106944 | tf_op jit(solution)/shard_map/while/body/eval_jaxpr/add | solution.py:35
  745.5 20.7 %multiply_add_fusion.9 = (f32[128,65,1,128]{3,0,2,1:T(8,128)}, f32[128,65,1,128]{3,0,2,1:T(8,128)}) fusion(f32[128,65,2,128]{3,0,2,1:T(8,128)} %get-tuple-element.855, s32[128]{0:T(128)S(1)} %get-tuple-element.771, s32[65,128]{1,0:T(8,128)S(1)} %get-tuple-element.772, s32[128]{0:T(128)S(1)} %get-tuple-element.773, ...), kind=kLoop, calls=%fused_computation.56.clone.1.clone | loop fusion | flops 23429120 | bytes 17106944 | tf_op jit(solution)/shard_map/while/body/eval_jaxpr/add | solution.py:35
  778.8 20.7 %multiply_add_fusion.9 = (f32[128,65,1,128]{3,0,2,1:T(8,128)}, f32[128,65,1,128]{3,0,2,1:T(8,128)}) fusion(f32[128,65,2,128]{3,0,2,1:T(8,128)} %get-tuple-element.855, s32[128]{0:T(128)S(1)} %get-tuple-element.771, s32[65,128]{1,0:T(8,128)S(1)} %get-tuple-element.772, s32[128]{0:T(128)S(1)} %get-tuple-element.773, ...), kind=kLoop, calls=%fused_computation.56.clone.1.clone | loop fusion | flops 23429120 | bytes 17106944 | tf_op jit(solution)/shard_map/while/body/eval_jaxpr/add | solution.py:35
  812.2 20.7 %multiply_add_fusion.9 = (f32[128,65,1,128]{3,0,2,1:T(8,128)}, f32[128,65,1,128]{3,0,2,1:T(8,128)}) fusion(f32[128,65,2,128]{3,0,2,1:T(8,128)} %get-tuple-element.855, s32[128]{0:T(128)S(1)} %get-tuple-element.771, s32[65,128]{1,0:T(8,128)S(1)} %get-tuple-element.772, s32[128]{0:T(128)S(1)} %get-tuple-element.773, ...), kind=kLoop, calls=%fused_computation.56.clone.1.clone | loop fusion | flops 23429120 | bytes 17106944 | tf_op jit(solution)/shard_map/while/body/eval_jaxpr/add | solution.py:35
  845.6 20.7 %multiply_add_fusion.9 = (f32[128,65,1,128]{3,0,2,1:T(8,128)}, f32[128,65,1,128]{3,0,2,1:T(8,128)}) fusion(f32[128,65,2,128]{3,0,2,1:T(8,128)} %get-tuple-element.855, s32[128]{0:T(128)S(1)} %get-tuple-element.771, s32[65,128]{1,0:T(8,128)S(1)} %get-tuple-element.772, s32[128]{0:T(128)S(1)} %get-tuple-element.773, ...), kind=kLoop, calls=%fused_computation.56.clone.1.clone | loop fusion | flops 23429120 | bytes 17106944 | tf_op jit(solution)/shard_map/while/body/eval_jaxpr/add | solution.py:35
  879.0 20.7 %multiply_add_fusion.9 = (f32[128,65,1,128]{3,0,2,1:T(8,128)}, f32[128,65,1,128]{3,0,2,1:T(8,128)}) fusion(f32[128,65,2,128]{3,0,2,1:T(8,128)} %get-tuple-element.855, s32[128]{0:T(128)S(1)} %get-tuple-element.771, s32[65,128]{1,0:T(8,128)S(1)} %get-tuple-element.772, s32[128]{0:T(128)S(1)} %get-tuple-element.773, ...), kind=kLoop, calls=%fused_computation.56.clone.1.clone | loop fusion | flops 23429120 | bytes 17106944 | tf_op jit(solution)/shard_map/while/body/eval_jaxpr/add | solution.py:35
  912.4 20.7 %multiply_add_fusion.9 = (f32[128,65,1,128]{3,0,2,1:T(8,128)}, f32[128,65,1,128]{3,0,2,1:T(8,128)}) fusion(f32[128,65,2,128]{3,0,2,1:T(8,128)} %get-tuple-element.855, s32[128]{0:T(128)S(1)} %get-tuple-element.771, s32[65,128]{1,0:T(8,128)S(1)} %get-tuple-element.772, s32[128]{0:T(128)S(1)} %get-tuple-element.773, ...), kind=kLoop, calls=%fused_computation.56.clone.1.clone | loop fusion | flops 23429120 | bytes 17106944 | tf_op jit(solution)/shard_map/while/body/eval_jaxpr/add | solution.py:35
  957.9 69.6 %scatter_fusion = f32[1040,3,8,128]{3,2,1,0:T(8,128)} fusion(f32[1040,3,8,128]{3,2,1,0:T(8,128)} %broadcast_in_dim.61, s32[520]{0:T(1024)S(1)} %fusion.92, f32[520,3,8,128]{3,2,1,0:T(8,128)} %pad_maximum_fusion), kind=kCustom, calls=%fused_computation.6 | custom fusion | bytes 19171360 | tf_op jit(solution)/shard_map/scatter | solution.py:147
  1033.9 126.7 %all-to-all-done.3 = f32[4,260,3,8,128]{4,3,2,1,0:T(8,128)} async-done(((f32[4,260,3,8,128]{4,3,2,1,0:T(8,128)}), f32[4,260,3,8,128]{4,3,2,1,0:T(8,128)}, u32[]{:S(2)}, u32[]{:S(2)}) %all-to-all-start.3) | async-done | bytes 12779552 | tf_op jit(solution)/shard_map/all_to_all | solution.py:151
  1160.6 182.0 %while.53 = (s32[]{:T(128)}, f32[4,260,3,8,128]{4,3,2,1,0:T(8,128)}, f32[4,260,3,8,128]{4,3,2,1,0:T(8,128)}, s32[4,260]{1,0:T(4,128)}, f32[64,128,128]{2,1,0:T(8,128)}) while((s32[]{:T(128)}, f32[4,260,3,8,128]{4,3,2,1,0:T(8,128)}, f32[4,260,3,8,128]{4,3,2,1,0:T(8,128)}, s32[4,260]{1,0:T(4,128)}, ...), condition=%wide.region_21.22_spmd.clone, body=%wide.region_20.21_spmd.sunk.clone | while | flops 1226835712 | bytes 57517184 | solution.py:152
  1176.2 30.2 %bitcast_dynamic-update-slice_fusion.7 = f32[4,260,3,8,128]{4,3,2,1,0:T(8,128)} fusion(f32[4,260,3,8,128]{4,3,2,1,0:T(8,128)} %get-tuple-element.867, s32[]{:T(128)} %get-tuple-element.866, f32[260,128,128]{2,1,0:T(8,128)} %gather_fusion.1, f32[4,260,3,8,128]{4,3,2,1,0:T(8,128)} %get-tuple-element.873), kind=kOutput, calls=%fused_computation.87.clone.1.clone | convolution fusion | flops 1226833920 | bytes 23430144 | tf_op jit(solution)/shard_map/while/body/eval_jaxpr/nmkq,nrq->nmkr/dot_general | solution.py:47
  1221.8 30.2 %bitcast_dynamic-update-slice_fusion.7 = f32[4,260,3,8,128]{4,3,2,1,0:T(8,128)} fusion(f32[4,260,3,8,128]{4,3,2,1,0:T(8,128)} %get-tuple-element.867, s32[]{:T(128)} %get-tuple-element.866, f32[260,128,128]{2,1,0:T(8,128)} %gather_fusion.1, f32[4,260,3,8,128]{4,3,2,1,0:T(8,128)} %get-tuple-element.873), kind=kOutput, calls=%fused_computation.87.clone.1.clone | convolution fusion | flops 1226833920 | bytes 23430144 | tf_op jit(solution)/shard_map/while/body/eval_jaxpr/nmkq,nrq->nmkr/dot_general | solution.py:47
  1267.1 30.2 %bitcast_dynamic-update-slice_fusion.7 = f32[4,260,3,8,128]{4,3,2,1,0:T(8,128)} fusion(f32[4,260,3,8,128]{4,3,2,1,0:T(8,128)} %get-tuple-element.867, s32[]{:T(128)} %get-tuple-element.866, f32[260,128,128]{2,1,0:T(8,128)} %gather_fusion.1, f32[4,260,3,8,128]{4,3,2,1,0:T(8,128)} %get-tuple-element.873), kind=kOutput, calls=%fused_computation.87.clone.1.clone | convolution fusion | flops 1226833920 | bytes 23430144 | tf_op jit(solution)/shard_map/while/body/eval_jaxpr/nmkq,nrq->nmkr/dot_general | solution.py:47
  1312.4 30.2 %bitcast_dynamic-update-slice_fusion.7 = f32[4,260,3,8,128]{4,3,2,1,0:T(8,128)} fusion(f32[4,260,3,8,128]{4,3,2,1,0:T(8,128)} %get-tuple-element.867, s32[]{:T(128)} %get-tuple-element.866, f32[260,128,128]{2,1,0:T(8,128)} %gather_fusion.1, f32[4,260,3,8,128]{4,3,2,1,0:T(8,128)} %get-tuple-element.873), kind=kOutput, calls=%fused_computation.87.clone.1.clone | convolution fusion | flops 1226833920 | bytes 23430144 | tf_op jit(solution)/shard_map/while/body/eval_jaxpr/nmkq,nrq->nmkr/dot_general | solution.py:47
  1351.3 144.0 %scatter_fusion.1 = f32[2080,3,8,128]{3,2,1,0:T(8,128)} fusion(f32[2080,3,8,128]{3,2,1,0:T(8,128)} %broadcast_in_dim.53, s32[1040]{0:T(1024)S(1)} %copy-done.7, f32[1040,3,8,128]{3,2,1,0:T(8,128)} %bitcast.202), kind=kCustom, calls=%fused_computation.7 | custom fusion | flops 3194880 | bytes 38342720 | tf_op jit(solution)/shard_map/scatter-add | solution.py:155
  1496.6 248.8 %reduce-scatter.2.cloned.1.call-done = f32[4,65,3,8,128]{4,3,2,1,0:T(8,128)} async-done(((f32[32,65,3,8,128]{4,3,2,1,0:T(8,128)}), f32[4,65,3,8,128]{4,3,2,1,0:T(8,128)}) %reduce-scatter.2.cloned.1.call-update) | async-done | bytes 3194896 | tf_op jit(solution)/shard_map/reduce_scatter | solution.py:157
  (245 shorter events, 513.7 us)
Async XLA Ops:
  16.5 10.7 all-to-all-start
  27.2 25.3 %all-to-all-start.1 = ((s32[4,1,260]{2,1,0:T(1,128)}), s32[4,1,260]{2,1,0:T(1,128)S(1)}, u32[]{:S(2)}, u32[]{:S(2)}) async-start(s32[4,1,260]{2,1,0:T(1,128)} %all_to_all.22), calls=%async_computation.1 | async-start | bytes 12288 | tf_op jit(solution)/shard_map/all_to_all | solution.py:94
  31.7 13.2 copy-start.6
  182.7 100.4 %all-to-all-start.2 = ((f32[4,260,2,8,128]{4,3,2,1,0:T(8,128)}), f32[4,260,2,8,128]{4,3,2,1,0:T(8,128)}, u32[]{:S(2)}, u32[]{:S(2)}) async-start(f32[4,260,2,8,128]{4,3,2,1,0:T(8,128)} %get-tuple-element.363), calls=%async_computation.2 | async-start | bytes 17039360 | tf_op jit(solution)/shard_map/all_to_all | solution.py:100
  188.8 8.1 slice-start
  188.8 8.1 slice-start.1
  188.8 8.1 slice-start.2
  196.9 4.6 copy-start.13
  196.9 4.6 copy-start.14
  196.9 4.6 copy-start.8
  289.6 3.5 copy-start.3
  297.9 19.7 %copy-start.1 = (f32[128,65,128]{2,0,1:T(8,128)S(1)}, f32[128,65,128]{2,0,1:T(8,128)}, u32[]{:S(2)}) copy-start(f32[128,65,128]{2,0,1:T(8,128)} %get-tuple-element.827) | copy-start | bytes 12779524 | tf_op jit(solution)/shard_map/while
  297.9 19.7 %copy-start.2 = (f32[8,65,2,8,128]{4,3,1,0,2:T(8,128)S(1)}, f32[8,65,2,8,128]{4,3,1,0,2:T(8,128)}, u32[]{:S(2)}) copy-start(f32[8,65,2,8,128]{4,3,1,0,2:T(8,128)} %get-tuple-element.831) | copy-start | bytes 12779524 | tf_op jit(solution)/shard_map/while
  329.4 19.7 %copy-start.1 = (f32[128,65,128]{2,0,1:T(8,128)S(1)}, f32[128,65,128]{2,0,1:T(8,128)}, u32[]{:S(2)}) copy-start(f32[128,65,128]{2,0,1:T(8,128)} %get-tuple-element.827) | copy-start | bytes 12779524 | tf_op jit(solution)/shard_map/while
  329.4 19.7 %copy-start.2 = (f32[8,65,2,8,128]{4,3,1,0,2:T(8,128)S(1)}, f32[8,65,2,8,128]{4,3,1,0,2:T(8,128)}, u32[]{:S(2)}) copy-start(f32[8,65,2,8,128]{4,3,1,0,2:T(8,128)} %get-tuple-element.831) | copy-start | bytes 12779524 | tf_op jit(solution)/shard_map/while
  360.8 19.7 %copy-start.1 = (f32[128,65,128]{2,0,1:T(8,128)S(1)}, f32[128,65,128]{2,0,1:T(8,128)}, u32[]{:S(2)}) copy-start(f32[128,65,128]{2,0,1:T(8,128)} %get-tuple-element.827) | copy-start | bytes 12779524 | tf_op jit(solution)/shard_map/while
  360.8 19.7 %copy-start.2 = (f32[8,65,2,8,128]{4,3,1,0,2:T(8,128)S(1)}, f32[8,65,2,8,128]{4,3,1,0,2:T(8,128)}, u32[]{:S(2)}) copy-start(f32[8,65,2,8,128]{4,3,1,0,2:T(8,128)} %get-tuple-element.831) | copy-start | bytes 12779524 | tf_op jit(solution)/shard_map/while
  392.2 19.7 %copy-start.1 = (f32[128,65,128]{2,0,1:T(8,128)S(1)}, f32[128,65,128]{2,0,1:T(8,128)}, u32[]{:S(2)}) copy-start(f32[128,65,128]{2,0,1:T(8,128)} %get-tuple-element.827) | copy-start | bytes 12779524 | tf_op jit(solution)/shard_map/while
  392.2 19.7 %copy-start.2 = (f32[8,65,2,8,128]{4,3,1,0,2:T(8,128)S(1)}, f32[8,65,2,8,128]{4,3,1,0,2:T(8,128)}, u32[]{:S(2)}) copy-start(f32[8,65,2,8,128]{4,3,1,0,2:T(8,128)} %get-tuple-element.831) | copy-start | bytes 12779524 | tf_op jit(solution)/shard_map/while
  423.7 19.7 %copy-start.1 = (f32[128,65,128]{2,0,1:T(8,128)S(1)}, f32[128,65,128]{2,0,1:T(8,128)}, u32[]{:S(2)}) copy-start(f32[128,65,128]{2,0,1:T(8,128)} %get-tuple-element.827) | copy-start | bytes 12779524 | tf_op jit(solution)/shard_map/while
  423.7 19.7 %copy-start.2 = (f32[8,65,2,8,128]{4,3,1,0,2:T(8,128)S(1)}, f32[8,65,2,8,128]{4,3,1,0,2:T(8,128)}, u32[]{:S(2)}) copy-start(f32[8,65,2,8,128]{4,3,1,0,2:T(8,128)} %get-tuple-element.831) | copy-start | bytes 12779524 | tf_op jit(solution)/shard_map/while
  455.1 19.7 %copy-start.1 = (f32[128,65,128]{2,0,1:T(8,128)S(1)}, f32[128,65,128]{2,0,1:T(8,128)}, u32[]{:S(2)}) copy-start(f32[128,65,128]{2,0,1:T(8,128)} %get-tuple-element.827) | copy-start | bytes 12779524 | tf_op jit(solution)/shard_map/while
  455.1 19.7 %copy-start.2 = (f32[8,65,2,8,128]{4,3,1,0,2:T(8,128)S(1)}, f32[8,65,2,8,128]{4,3,1,0,2:T(8,128)}, u32[]{:S(2)}) copy-start(f32[8,65,2,8,128]{4,3,1,0,2:T(8,128)} %get-tuple-element.831) | copy-start | bytes 12779524 | tf_op jit(solution)/shard_map/while
  486.6 19.7 %copy-start.1 = (f32[128,65,128]{2,0,1:T(8,128)S(1)}, f32[128,65,128]{2,0,1:T(8,128)}, u32[]{:S(2)}) copy-start(f32[128,65,128]{2,0,1:T(8,128)} %get-tuple-element.827) | copy-start | bytes 12779524 | tf_op jit(solution)/shard_map/while
  486.6 19.7 %copy-start.2 = (f32[8,65,2,8,128]{4,3,1,0,2:T(8,128)S(1)}, f32[8,65,2,8,128]{4,3,1,0,2:T(8,128)}, u32[]{:S(2)}) copy-start(f32[8,65,2,8,128]{4,3,1,0,2:T(8,128)} %get-tuple-element.831) | copy-start | bytes 12779524 | tf_op jit(solution)/shard_map/while
  518.0 19.7 %copy-start.1 = (f32[128,65,128]{2,0,1:T(8,128)S(1)}, f32[128,65,128]{2,0,1:T(8,128)}, u32[]{:S(2)}) copy-start(f32[128,65,128]{2,0,1:T(8,128)} %get-tuple-element.827) | copy-start | bytes 12779524 | tf_op jit(solution)/shard_map/while
  518.0 19.7 %copy-start.2 = (f32[8,65,2,8,128]{4,3,1,0,2:T(8,128)S(1)}, f32[8,65,2,8,128]{4,3,1,0,2:T(8,128)}, u32[]{:S(2)}) copy-start(f32[8,65,2,8,128]{4,3,1,0,2:T(8,128)} %get-tuple-element.831) | copy-start | bytes 12779524 | tf_op jit(solution)/shard_map/while
  549.4 19.7 %copy-start.1 = (f32[128,65,128]{2,0,1:T(8,128)S(1)}, f32[128,65,128]{2,0,1:T(8,128)}, u32[]{:S(2)}) copy-start(f32[128,65,128]{2,0,1:T(8,128)} %get-tuple-element.827) | copy-start | bytes 12779524 | tf_op jit(solution)/shard_map/while
  549.5 19.7 %copy-start.2 = (f32[8,65,2,8,128]{4,3,1,0,2:T(8,128)S(1)}, f32[8,65,2,8,128]{4,3,1,0,2:T(8,128)}, u32[]{:S(2)}) copy-start(f32[8,65,2,8,128]{4,3,1,0,2:T(8,128)} %get-tuple-element.831) | copy-start | bytes 12779524 | tf_op jit(solution)/shard_map/while
  1027.5 133.1 %all-to-all-start.3 = ((f32[4,260,3,8,128]{4,3,2,1,0:T(8,128)}), f32[4,260,3,8,128]{4,3,2,1,0:T(8,128)}, u32[]{:S(2)}, u32[]{:S(2)}) async-start(f32[4,260,3,8,128]{4,3,2,1,0:T(8,128)} %bitcast.196), calls=%async_computation.3 | async-start | bytes 25559040 | tf_op jit(solution)/shard_map/all_to_all | solution.py:151
  1033.8 711.5 %reduce-scatter.2.cloned.1.call-start = ((), (), s32[]{:S(2)}) async-start(), calls=%async_computation.5 | async-start | bytes 28753920 | tf_op jit(solution)/shard_map/reduce_scatter | solution.py:157
  1342.6 8.7 copy-start.7
  (7 other events, 8.9 us)
Sparse Core Ops, SparseCore 0:
  1495.5 249.8 reduce-scatter.1
